TPU v7x, 32 devices: a whole 2x2x4 slice. The times are simulated.
32 devices in a mesh: dp: 2 (over y), fsdp: 4 (over x, core), tensor: 4 (over z).
Axes of the slice: x: 2, y: 2, z: 4, core: 2. Of those that a mesh axis runs over, the one named last changes fastest.
Arguments:
- activations: bfloat16 [1024, 8192], P(('dp', 'fsdp'), 'tensor'), may hold values from -6 to 6
- cotangent: bfloat16 [1024, 8192], P(('dp', 'fsdp'), 'tensor'), may hold values from -6 to 6
- up_tiles: bfloat16 [1024, 128, 128], P(('fsdp', 'tensor')), may hold values from -0.1875 to 0.1875
- down_tiles: bfloat16 [1024, 128, 128], P(('fsdp', 'tensor')), may hold values from -0.125 to 0.125
- up_rows: int32 [256, 4], P(None, 'tensor'), may hold values from 0 to 63, as said below
- up_cols: int32 [256, 4], P(None, 'tensor'), may hold values from 0 to 31, as said below
- down_rows: int32 [256, 4], P(None, 'tensor'), may hold values from 0 to 31, as said below
- down_cols: int32 [256, 4], P(None, 'tensor'), may hold values from 0 to 63, as said below
Outputs:
- output: bfloat16 [1024, 8192], P(('dp', 'fsdp'), 'tensor')
- input_grad: bfloat16 [1024, 8192], P(('dp', 'fsdp'), 'tensor')
- up_grad: float32 [1024, 128, 128], P(('fsdp', 'tensor'))
- down_grad: float32 [1024, 128, 128], P(('fsdp', 'tensor'))
Inputs may be any that keep to these rules, and one draw needn't show every extreme that they name: `up_rows`: within a column, the up tiles of one hidden-unit block name distinct feature blocks. `up_cols`: every value occurs exactly 8 times in each column. `down_rows`: every value occurs exactly 8 times in each column. `down_cols`: within a column, the down tiles of one hidden-unit block name distinct feature blocks.
All inputs are finite; a program needn't handle non-finite values.
Results may differ from a plain program's by a relative error of at most 0.018.
Values may be sent and summed in bfloat16 or wider, within the bound.
A program may use at most 128 MiB of HBM per device.

v0:
```python
import jax
import jax.numpy as jnp
from jax import lax
from jax.sharding import PartitionSpec as P

D = 8192
FF = 16384
inv_root_two = 0.7071067811865476
inv_root_tau = 0.3989422804014327


def gelu_parts(values):
    normal_cdf = 0.5 * (1.0 + jax.scipy.special.erf(values * inv_root_two))
    density = inv_root_tau * jnp.exp(-0.5 * values * values)
    return (values * normal_cdf, normal_cdf + values * density)


def grouped_pick(acting, far_index, hidden_blocks, block_size):
    rows_here = acting.shape[0]
    picked = acting.reshape(rows_here, -1, block_size)[:, far_index]
    return picked.reshape(rows_here, hidden_blocks, -1, block_size)


def add_far(product, far_index, model_blocks):
    rows_here = product.shape[0]
    block_size = product.shape[-1]
    flat = product.reshape(rows_here, -1, block_size)
    summed = (
        jnp.zeros((rows_here, model_blocks, block_size), jnp.float32).at[:, far_index].add(flat)
    )
    return summed.reshape(rows_here, model_blocks * block_size)


def grouped_tiles(tiles, order, hidden_blocks):
    block_size = tiles.shape[1]
    return tiles[order].reshape(hidden_blocks, -1, block_size, block_size)


def body(activations, cotangent, up_tiles, down_tiles, up_rows, up_cols, down_rows, down_cols):
    block_size = up_tiles.shape[1]
    hidden_blocks = FF // (block_size * lax.axis_size("tensor"))
    model_blocks = D // block_size
    up_order = jnp.argsort(up_cols[:, 0], stable=True)
    down_order = jnp.argsort(down_rows[:, 0], stable=True)
    up_back = jnp.argsort(up_order)
    down_back = jnp.argsort(down_order)
    up_far = up_rows[:, 0][up_order]
    down_far = down_cols[:, 0][down_order]
    full_input = lax.all_gather(activations, "tensor", axis=1, tiled=True)
    input_pick = grouped_pick(full_input, up_far, hidden_blocks, block_size)
    up_whole = lax.all_gather(up_tiles, "fsdp", axis=0, tiled=True)
    up_sorted = grouped_tiles(up_whole, up_order, hidden_blocks)
    pre_act = jnp.einsum(
        "thkb,hkbc->thc", input_pick, up_sorted, preferred_element_type=jnp.float32
    )
    gelu_out, gelu_slope = gelu_parts(pre_act)
    hidden = gelu_out.astype(jnp.bfloat16)
    down_whole = lax.all_gather(down_tiles, "fsdp", axis=0, tiled=True)
    down_sorted = grouped_tiles(down_whole, down_order, hidden_blocks)
    out_product = jnp.einsum(
        "thb,hkbc->thkc", hidden, down_sorted, preferred_element_type=jnp.float32
    )
    partial_out = add_far(out_product, down_far, model_blocks)
    output = lax.psum_scatter(
        partial_out.astype(jnp.bfloat16), "tensor", scatter_dimension=1, tiled=True
    )
    full_cotangent = lax.all_gather(cotangent, "tensor", axis=1, tiled=True)
    cot_pick = grouped_pick(full_cotangent, down_far, hidden_blocks, block_size)
    hidden_grad = jnp.einsum(
        "thkc,hkbc->thb", cot_pick, down_sorted, preferred_element_type=jnp.float32
    )
    pre_grad = (hidden_grad * gelu_slope).astype(jnp.bfloat16)
    in_product = jnp.einsum(
        "thc,hkbc->thkb", pre_grad, up_sorted, preferred_element_type=jnp.float32
    )
    partial_in = add_far(in_product, up_far, model_blocks)
    input_grad = lax.psum_scatter(
        partial_in.astype(jnp.bfloat16), "tensor", scatter_dimension=1, tiled=True
    )
    up_grouped = jnp.einsum(
        "thkb,thc->hkbc", input_pick, pre_grad, preferred_element_type=jnp.float32
    )
    down_grouped = jnp.einsum(
        "thb,thkc->hkbc", hidden, cot_pick, preferred_element_type=jnp.float32
    )
    up_rounded = up_grouped.astype(jnp.bfloat16).reshape(-1, block_size, block_size)
    down_rounded = down_grouped.astype(jnp.bfloat16).reshape(-1, block_size, block_size)
    up_term = up_rounded[up_back].astype(jnp.float32)
    down_term = down_rounded[down_back].astype(jnp.float32)
    replicas = lax.axis_size("dp")
    owners = lax.axis_size("fsdp")

    def regroup(grad_term):
        per_piece = grad_term.shape[0] // (replicas * owners)
        shaped = grad_term.reshape(owners, replicas, per_piece, block_size, block_size)
        return shaped.transpose(1, 0, 2, 3, 4).reshape(-1, block_size, block_size)

    up_piece, down_piece = (
        lax.psum_scatter(
            regroup(up_term).astype(jnp.bfloat16), ("dp", "fsdp"), scatter_dimension=0, tiled=True
        ).astype(jnp.float32),
        lax.psum_scatter(
            regroup(down_term).astype(jnp.bfloat16), ("dp", "fsdp"), scatter_dimension=0, tiled=True
        ).astype(jnp.float32),
    )
    up_grad, down_grad = (
        lax.all_gather(up_piece.astype(jnp.bfloat16), "dp", axis=0, tiled=True).astype(
            up_piece.dtype
        ),
        lax.all_gather(down_piece.astype(jnp.bfloat16), "dp", axis=0, tiled=True).astype(
            down_piece.dtype
        ),
    )
    return (output, input_grad, up_grad, down_grad)


def solution(mesh):
    in_specs = (
        P(("dp", "fsdp"), "tensor"),
        P(("dp", "fsdp"), "tensor"),
        P(("fsdp", "tensor"), None, None),
        P(("fsdp", "tensor"), None, None),
        P(None, "tensor"),
        P(None, "tensor"),
        P(None, "tensor"),
        P(None, "tensor"),
    )
    out_specs = (
        P(("dp", "fsdp"), "tensor"),
        P(("dp", "fsdp"), "tensor"),
        P(("fsdp", "tensor"), None, None),
        P(("fsdp", "tensor"), None, None),
    )
    return jax.shard_map(body, mesh=mesh, in_specs=in_specs, out_specs=out_specs, check_vma=False)
```

profile of v0, /device:TPU:0, one launch (start us, length us, event | category | flops | bytes accessed | tf_op | source)
XLA Modules:
  0.0 582.8 jit_solution(14450266587126344888)
XLA Ops:
  7.2 0.0 all-gather.11.cloned.1.call-start
  7.2 2.0 copy.62
  9.3 0.0 all-gather.11.cloned.1.call-update
  9.3 0.0 all-gather.13.cloned.1.call-start
  9.4 2.0 copy.69
  11.4 0.0 all-gather.13.cloned.1.call-update
  11.4 0.0 all-gather.9.cloned.1.call-start
  11.5 0.7 all-gather.9.cloned.1.call-update
  12.2 0.0 all-gather.7.cloned.1.call-start
  12.2 0.5 all-gather.7.cloned.1.call-update
  12.7 0.0 reduce-scatter.11.cloned.1.call-start
  12.8 3.8 sort.62
  16.6 3.2 sort.65
  19.8 3.8 sort.63
  23.7 1.9 gather_fusion.3
  25.7 1.9 gather_fusion
  27.7 32.2 %all-gather.11.cloned.1.call-done = bf16[128,8192]{0,1:T(8,128)(2,1)} async-done(((bf16[128,2048]{0,1:T(8,128)(2,1)}), bf16[128,8192]{0,1:T(8,128)(2,1)}) %all-gather.11.cloned.1.call-update) | async-done | bytes 2097168 | tf_op jit(solution)/shard_map/all_gather | solution.py:49
  59.9 3.2 copy.63
  63.1 43.5 %all-gather.13.cloned.1.call-done = bf16[128,8192]{0,1:T(8,128)(2,1)} async-done(((bf16[128,2048]{0,1:T(8,128)(2,1)}), bf16[128,8192]{0,1:T(8,128)(2,1)}) %all-gather.13.cloned.1.call-update) | async-done | bytes 2097168 | tf_op jit(solution)/shard_map/all_gather | solution.py:67
  106.6 4.1 copy.70
  110.7 10.3 %gather_fusion.5 = bf16[256,128,128]{2,1,0:T(8,128)(2,1)} fusion(bf16[128,64,128]{2,0,1:T(8,128)(2,1)} %copy.70, s32[1024]{0:T(1024)S(1)} %pad_clamp_fusion.2), kind=kCustom, calls=%fused_computation.5 | custom fusion | bytes 16778240 | tf_op jit(solution)/shard_map/gather | solution.py:20
  121.0 8.6 %gather_fusion.4 = bf16[256,128,128]{2,1,0:T(8,128)(2,1)} fusion(bf16[128,64,128]{2,0,1:T(8,128)(2,1)S(1)} %copy.63, s32[1024]{0:T(1024)S(1)} %pad_clamp_fusion.3), kind=kCustom, calls=%fused_computation.4 | custom fusion | bytes 16778240 | tf_op jit(solution)/shard_map/gather | solution.py:20
  129.6 35.7 %all-gather.9.cloned.1.call-done = bf16[256,128,128]{2,1,0:T(8,128)(2,1)} async-done(((bf16[64,128,128]{2,1,0:T(8,128)(2,1)}), bf16[256,128,128]{2,1,0:T(8,128)(2,1)}) %all-gather.9.cloned.1.call-update) | async-done | bytes 8388624 | tf_op jit(solution)/shard_map/all_gather | solution.py:51
  165.3 13.5 %gather_fusion.2 = bf16[256,128,128]{2,1,0:T(8,128)(2,1)} fusion(bf16[256,128,128]{2,1,0:T(8,128)(2,1)} %all-gather.9.cloned.1.call-done, s32[1024]{0:T(1024)S(1)} %pad_clamp_fusion.4), kind=kCustom, calls=%fused_computation.2 | custom fusion | bytes 16778240 | tf_op jit(solution)/shard_map/gather | solution.py:36
  178.8 8.3 %fusion.15 = f32[32,128,128,1]{2,1,3,0:T(8,128)S(1)} fusion(bf16[32,8,128,128]{3,2,1,0:T(8,128)(2,1)} %bitcast.97, bf16[128,32,8,128]{3,0,2,1:T(8,128)(2,1)} %bitcast.99), kind=kOutput, calls=%fused_computation.40 | convolution fusion | flops 1073741824 | bytes 18874368 | tf_op jit(solution)/shard_map/thkb,hkbc->thc/dot_general | solution.py:53
  187.1 9.3 %convolution_convert_fusion = bf16[32,8,128,128]{3,2,1,0:T(8,128)(2,1)} fusion(bf16[128,32,8,128]{3,0,2,1:T(8,128)(2,1)} %bitcast.106, f32[32,128,128,1]{2,1,3,0:T(8,128)S(1)} %fusion.15), kind=kOutput, calls=%fused_computation.10 | convolution fusion | flops 1080557568 | bytes 18874368 | tf_op jit(solution)/shard_map/thb,thkc->hkbc/dot_general | solution.py:83
  196.5 12.1 %gather_fusion.7 = bf16[256,128,128]{1,2,0:T(8,128)(2,1)} fusion(bf16[256,128,128]{1,2,0:T(8,128)(2,1)} %bitcast.113, s32[1024]{0:T(1024)S(1)} %pad_clamp_fusion), kind=kCustom, calls=%fused_computation.7 | custom fusion | bytes 16778240 | tf_op jit(solution)/shard_map/gather | solution.py:89
  208.5 12.0 %copy.79 = bf16[4,2,32,128,128]{4,3,2,0,1:T(8,128)(2,1)} copy(bf16[4,2,32,128,128]{3,4,2,1,0:T(8,128)(2,1)} %bitcast.110) | data formatting | bytes 16777216 | tf_op jit(solution)/shard_map/convert_element_type | solution.py:103
  220.5 0.0 reduce-scatter.9.cloned.1.call-start
  220.6 3.2 sort.64
  223.8 1.2 all-gather.7.cloned.1.call-done
  225.0 12.7 %gather_fusion.1 = bf16[256,128,128]{2,1,0:T(8,128)(2,1)} fusion(bf16[256,128,128]{2,1,0:T(8,128)(2,1)} %all-gather.7.cloned.1.call-done, s32[1024]{0:T(1024)S(1)} %pad_clamp_fusion.5), kind=kCustom, calls=%fused_computation.1 | custom fusion | bytes 16778240 | tf_op jit(solution)/shard_map/gather | solution.py:36
  237.7 10.7 %fusion.10 = bf16[128,32,128,1]{0,2,3,1:T(8,128)(2,1)S(1)} fusion(f32[32,128,128,1]{2,1,3,0:T(8,128)S(1)} %fusion.15, bf16[32,8,128,128]{3,2,1,0:T(8,128)(2,1)} %bitcast.108, bf16[128,32,8,128]{3,0,2,1:T(8,128)(2,1)} %bitcast.107), kind=kOutput, calls=%fused_computation.25 | convolution fusion | flops 1078984704 | bytes 19922944 | tf_op jit(solution)/shard_map/thkc,hkbc->thb/dot_general | solution.py:69
  248.4 9.1 %convolution_convert_fusion.1 = bf16[32,8,128,128]{3,2,1,0:T(8,128)(2,1)} fusion(bf16[128,32,8,128]{3,0,2,1:T(8,128)(2,1)} %bitcast.100, bf16[128,32,128,1]{0,2,3,1:T(8,128)(2,1)S(1)} %fusion.10), kind=kOutput, calls=%fused_computation.11 | convolution fusion | flops 1077936128 | bytes 17825792 | tf_op jit(solution)/shard_map/thkb,thc->hkbc/dot_general | solution.py:80
  257.5 12.2 %gather_fusion.6 = bf16[256,128,128]{2,1,0:T(8,128)(2,1)} fusion(bf16[256,128,128]{2,1,0:T(8,128)(2,1)} %bitcast.111, s32[1024]{0:T(1024)S(1)} %pad_clamp_fusion.1), kind=kCustom, calls=%fused_computation.6 | custom fusion | bytes 16778240 | tf_op jit(solution)/shard_map/gather | solution.py:88
  269.7 10.4 %copy.76 = bf16[4,2,32,128,128]{4,3,2,0,1:T(8,128)(2,1)} copy(bf16[4,2,32,128,128]{4,3,2,1,0:T(8,128)(2,1)} %bitcast.112) | data formatting | bytes 16777216 | tf_op jit(solution)/shard_map/convert_element_type | solution.py:100
  280.1 0.3 reduce-scatter.5.cloned.1.call-start
  280.4 11.6 %fusion.13 = f32[32,8,128,128]{3,2,1,0:T(8,128)} fusion(bf16[32,8,128,128]{3,2,1,0:T(8,128)(2,1)} %bitcast.109, f32[32,128,128,1]{2,1,3,0:T(8,128)S(1)} %fusion.15), kind=kOutput, calls=%fused_computation.39 | convolution fusion | flops 1076363264 | bytes 27262976 | tf_op jit(solution)/shard_map/thb,hkbc->thkc/dot_general | solution.py:60
  292.0 17.5 %copy.67 = f32[128,256,128]{2,0,1:T(8,128)} copy(f32[128,256,128]{0,2,1:T(8,128)} %bitcast.103) | data formatting | bytes 33554432 | tf_op jit(solution)/shard_map/reshape | solution.py:27
  309.5 2.8 broadcast.42.clone
  312.2 52.3 %scatter_fusion = f32[128,64,128]{2,0,1:T(8,128)} fusion(f32[128,64,128]{2,0,1:T(8,128)} %broadcast.42.clone, s32[256]{0:T(256)S(1)} %bitcast.121, f32[256,128,128]{2,1,0:T(8,128)} %bitcast.102), kind=kCustom, calls=%fused_computation.8 | custom fusion | flops 4194304 | bytes 50332672 | tf_op jit(solution)/shard_map/scatter-add | solution.py:29
  364.6 2.6 convert_element_type.64
  367.2 2.9 copy.68
  370.1 0.0 reduce-scatter.7.cloned.1.call-start
  370.1 11.5 %fusion.16 = f32[32,8,128,128]{3,2,1,0:T(8,128)} fusion(bf16[32,8,128,128]{3,2,1,0:T(8,128)(2,1)} %bitcast.98, bf16[128,32,128,1]{0,2,3,1:T(8,128)(2,1)S(1)} %fusion.10), kind=kOutput, calls=%fused_computation.41 | convolution fusion | flops 1073741824 | bytes 26214400 | tf_op jit(solution)/shard_map/thc,hkbc->thkb/dot_general | solution.py:73
  381.6 17.5 %copy.72 = f32[128,256,128]{2,0,1:T(8,128)} copy(f32[128,256,128]{0,2,1:T(8,128)} %bitcast.96) | data formatting | bytes 33554432 | tf_op jit(solution)/shard_map/reshape | solution.py:27
  399.1 2.5 broadcast.42.clone.1
  401.7 51.3 %scatter_fusion.1 = f32[128,64,128]{2,0,1:T(8,128)} fusion(f32[128,64,128]{2,0,1:T(8,128)} %broadcast.42.clone.1, s32[256]{0:T(256)S(1)} %bitcast.119, f32[256,128,128]{2,1,0:T(8,128)} %bitcast.101), kind=kCustom, calls=%fused_computation.9 | custom fusion | flops 4194304 | bytes 50332672 | tf_op jit(solution)/shard_map/scatter-add | solution.py:29
  453.0 2.6 convert_element_type.67
  455.5 2.9 copy.73
  458.5 0.0 all-gather.17.cloned.1.call-start
  458.5 0.0 reduce-scatter.11.cloned.1.call-done
  458.5 0.6 all-gather.17.cloned.1.call-update
  459.2 0.0 all-gather.15.cloned.1.call-start
  459.2 0.0 reduce-scatter.9.cloned.1.call-done
  459.3 0.5 all-gather.15.cloned.1.call-update
  459.8 0.0 reduce-scatter.5.cloned.1.call-done
  459.8 2.0 copy.80
  461.9 41.3 %reduce-scatter.7.cloned.1.call-done = bf16[128,2048]{0,1:T(8,128)(2,1)} async-done(((bf16[128,8192]{0,1:T(8,128)(2,1)}), bf16[128,2048]{0,1:T(8,128)(2,1)}) %reduce-scatter.7.cloned.1.call-update) | async-done | bytes 524304 | tf_op jit(solution)/shard_map/reduce_scatter | solution.py:77
  503.2 2.0 copy.81
  505.2 31.8 %all-gather.17.cloned.1.call-done = bf16[64,128,128]{2,1,0:T(8,128)(2,1)} async-done(((bf16[32,128,128]{2,1,0:T(8,128)(2,1)}), bf16[64,128,128]{2,1,0:T(8,128)(2,1)}) %all-gather.17.cloned.1.call-update) | async-done | bytes 2097168 | tf_op jit(solution)/shard_map/all_gather | solution.py:110
  537.1 4.1 convert_element_type.79
  541.2 30.4 %all-gather.15.cloned.1.call-done = bf16[64,128,128]{2,1,0:T(8,128)(2,1)} async-done(((bf16[32,128,128]{2,1,0:T(8,128)(2,1)}), bf16[64,128,128]{2,1,0:T(8,128)(2,1)}) %all-gather.15.cloned.1.call-update) | async-done | bytes 2097168 | tf_op jit(solution)/shard_map/all_gather | solution.py:107
  571.6 4.1 convert_element_type.73
  (26 shorter events, 0.2 us)
Async XLA Ops:
  7.2 16.5 %copy-start = (s32[256,1]{0,1:T(1,128)S(1)}, s32[256,1]{0,1:T(1,128)}, u32[]{:S(2)}) copy-start(s32[256,1]{0,1:T(1,128)} %param.12) | copy-start | bytes 3076
  7.2 18.5 %copy-start.2 = (s32[256,1]{0,1:T(1,128)S(1)}, s32[256,1]{0,1:T(1,128)}, u32[]{:S(2)}) copy-start(s32[256,1]{0,1:T(1,128)} %param.15) | copy-start | bytes 3076
  7.2 52.7 %all-gather.11.cloned.1.call-start = ((), (), s32[]{:S(2)}) async-start(), calls=%async_computation.6 | async-start | bytes 2621440 | tf_op jit(solution)/shard_map/all_gather | solution.py:49
  9.3 97.3 %all-gather.13.cloned.1.call-start = ((), (), s32[]{:S(2)}) async-start(), calls=%async_computation.8 | async-start | bytes 2621440 | tf_op jit(solution)/shard_map/all_gather | solution.py:67
  11.4 153.9 %all-gather.9.cloned.1.call-start = ((), (), s32[]{:S(2)}) async-start(), calls=%async_computation.5 | async-start | bytes 10485760 | tf_op jit(solution)/shard_map/all_gather | solution.py:51
  12.2 212.8 %all-gather.7.cloned.1.call-start = ((), (), s32[]{:S(2)}) async-start(), calls=%async_computation.4 | async-start | bytes 10485760 | tf_op jit(solution)/shard_map/all_gather | solution.py:58
  12.7 445.8 %reduce-scatter.11.cloned.1.call-start = ((), (), s32[]{:S(2)}) async-start(), calls=%async_computation.12 | async-start | bytes 9437184 | tf_op jit(solution)/shard_map/reduce_scatter | solution.py:102
  220.5 238.7 %reduce-scatter.9.cloned.1.call-start = ((), (), s32[]{:S(2)}) async-start(), calls=%async_computation.10 | async-start | bytes 9437184 | tf_op jit(solution)/shard_map/reduce_scatter | solution.py:99
  280.1 179.7 %reduce-scatter.5.cloned.1.call-start = ((), (), s32[]{:S(2)}) async-start(), calls=%async_computation.7 | async-start | bytes 2621440 | tf_op jit(solution)/shard_map/reduce_scatter | solution.py:64
  370.1 133.1 %reduce-scatter.7.cloned.1.call-start = ((), (), s32[]{:S(2)}) async-start(), calls=%async_computation.9 | async-start | bytes 2621440 | tf_op jit(solution)/shard_map/reduce_scatter | solution.py:77
  458.5 78.6 %all-gather.17.cloned.1.call-start = ((), (), s32[]{:S(2)}) async-start(), calls=%async_computation.13 | async-start | bytes 3145728 | tf_op jit(solution)/shard_map/all_gather | solution.py:110
  458.5 117.2 %copy-start.1 = (s32[256,1]{0,1:T(1,128)S(1)}, s32[256,1]{0,1:T(1,128)}, u32[]{:S(2)}) copy-start(s32[256,1]{0,1:T(1,128)} %param.12) | copy-start | bytes 3076
  459.2 112.4 %all-gather.15.cloned.1.call-start = ((), (), s32[]{:S(2)}) async-start(), calls=%async_computation.11 | async-start | bytes 3145728 | tf_op jit(solution)/shard_map/all_gather | solution.py:107
Sparse Core Ops, SparseCore 0:
  10.1 49.7 all-gather.10
  62.1 44.5 all-gather.12
  108.2 57.0 all-gather.8
  166.7 58.2 all-gather.6
  228.3 71.5 reduce-scatter.10
  303.3 71.5 reduce-scatter.8
  377.7 43.6 reduce-scatter.4
  458.6 44.5 reduce-scatter.6
  504.7 32.2 all-gather.16
  538.5 33.0 all-gather.14
where the time goes:
time: 593 us; the launch traced here: 583 us
  waiting for transfers between devices  219 us (37%)
  local copies, waits for them, and re-layouts  157 us (26%)
  other arithmetic  131 us (22%)
  matrix products  60.6 us (10%)
  between operations  14.6 us (2%)
    scatter-add x2, other arithmetic, add_far(): jnp.zeros((rows_here, model_blocks, block_size), jnp.float32)  104 us
    all_gather x1, waiting for transfers between devices, body(): full_cotangent = lax.all_gather(cotangent, 'tensor', axis=1, tiled=True)  43.5 us
    reduce_scatter x1, waiting for transfers between devices, body(): lax.psum_scatter(partial_in.astype(jnp.bfloat16), 'tensor', scatter_dimen...  41.3 us
    all_gather x1, waiting for transfers between devices, body(): up_whole = lax.all_gather(up_tiles, 'fsdp', axis=0, tiled=True)  35.7 us
    reshape x2, local copies, waits for them, and re-layouts, add_far(): flat = product.reshape(rows_here, -1, block_size)  35 us
    all_gather x1, waiting for transfers between devices, body(): full_input = lax.all_gather(activations, 'tensor', axis=1, tiled=True)  32.2 us
    all_gather x1, waiting for transfers between devices, body(): lax.all_gather(down_piece.astype(jnp.bfloat16), 'dp', axis=0, tiled=True)  31.8 us
    all_gather x1, waiting for transfers between devices, body(): lax.all_gather(up_piece.astype(jnp.bfloat16), 'dp', axis=0, tiled=True)  30.4 us
  transfers between devices with their start and end apart: 10, of which 7 were waited for; matrix products, arithmetic and copies ran while one was open for 59% of the time, Pallas kernels for 0%

commit v1 on v0

--- a/solution.py
+++ b/solution.py
@@ -64,7 +64,14 @@
     output = lax.psum_scatter(
         partial_out.astype(jnp.bfloat16), "tensor", scatter_dimension=1, tiled=True
     )
-    full_cotangent = lax.all_gather(cotangent, "tensor", axis=1, tiled=True)
+    ring = [cotangent]
+    for hop in range(3):
+        ring.append(lax.ppermute(ring[-1], "tensor", [(dev, (dev + 1) % 4) for dev in range(4)]))
+    full_cotangent = jnp.roll(
+        jnp.concatenate(ring[::-1], axis=1),
+        (lax.axis_index("tensor") + 1) * ring[0].shape[1],
+        axis=1,
+    )
     cot_pick = grouped_pick(full_cotangent, down_far, hidden_blocks, block_size)
     hidden_grad = jnp.einsum(
         "thkc,hkbc->thb", cot_pick, down_sorted, preferred_element_type=jnp.float32

time: 593 us -> 563 us (0.949)
  waiting for transfers between devices: 219 us -> 172 us
  starting transfers between devices: 0.61 us -> 20.4 us
    all_gather x1 -> x0, waiting for transfers between devices: 43.5 us -> none  [body(): full_cotangent = lax.all_gather(cotangent, 'tensor', axis=1, tiled=True)]
    ppermute x0 -> x3, waiting for transfers between devices: none -> 36.8 us  [body(): lax.ppermute(ring[-1], 'tensor', [(dev, (dev + 1) % 4) for dev in range(4)])]
    all_gather x1, waiting for transfers between devices: 32.2 us -> 0.01 us  [body(): full_input = lax.all_gather(activations, 'tensor', axis=1, tiled=True)]
    ppermute x0 -> x3, starting transfers between devices: none -> 19.8 us  [body(): lax.ppermute(ring[-1], 'tensor', [(dev, (dev + 1) % 4) for dev in range(4)])]
    all_gather x1, waiting for transfers between devices: 35.7 us -> 24.3 us  [body(): up_whole = lax.all_gather(up_tiles, 'fsdp', axis=0, tiled=True)]
  transfers between devices with their start and end apart: 10 -> 12, of which waited for: 7 -> 8; matrix products, arithmetic and copies ran while one was open for 59% -> 62% of each run, Pallas kernels for 0% -> 0%
where the time goes in v1:
time: 563 us; the launch traced here: 552 us
  waiting for transfers between devices  172 us (31%)
  local copies, waits for them, and re-layouts  155 us (28%)
  other arithmetic  130 us (23%)
  matrix products  60.6 us (11%)
  starting transfers between devices  20.4 us (4%)
  between operations  14.3 us (3%)
    scatter-add x2, other arithmetic, add_far(): jnp.zeros((rows_here, model_blocks, block_size), jnp.float32)  104 us
    reduce_scatter x1, waiting for transfers between devices, body(): lax.psum_scatter(partial_in.astype(jnp.bfloat16), 'tensor', scatter_dimen...  40.6 us
    ppermute x3, waiting for transfers between devices, body(): lax.ppermute(ring[-1], 'tensor', [(dev, (dev + 1) % 4) for dev in range(4)])  36.8 us
    reshape x2, local copies, waits for them, and re-layouts, add_far(): flat = product.reshape(rows_here, -1, block_size)  35.1 us
    all_gather x1, waiting for transfers between devices, body(): lax.all_gather(down_piece.astype(jnp.bfloat16), 'dp', axis=0, tiled=True)  31.9 us
    all_gather x1, waiting for transfers between devices, body(): lax.all_gather(up_piece.astype(jnp.bfloat16), 'dp', axis=0, tiled=True)  30.5 us
    gather x2, local copies, waits for them, and re-layouts, grouped_tiles(): return tiles[order].reshape(hidden_blocks, -1, block_size, block_size)  26.1 us
    all_gather x1, waiting for transfers between devices, body(): up_whole = lax.all_gather(up_tiles, 'fsdp', axis=0, tiled=True)  24.3 us
  transfers between devices with their start and end apart: 12, of which 8 were waited for; matrix products, arithmetic and copies ran while one was open for 62% of the time, Pallas kernels for 0%

profile of v1, /device:TPU:0, one launch (start us, length us, event | category | flops | bytes accessed | tf_op | source)
XLA Modules:
  0.0 552.3 jit_solution(6361769145240228448)
XLA Ops:
  7.3 2.1 copy.63
  9.4 0.7 all-gather.8.cloned.1.call-update
  10.2 0.7 all-gather.6.cloned.1.call-update
  10.9 0.3 copy.70
  11.2 3.1 collective-permute-start
  14.3 3.2 sort.62
  17.5 3.2 sort.65
  20.7 3.2 sort.63
  23.8 3.2 sort.64
  27.0 1.9 gather_fusion
  29.0 0.7 collective-permute-done
  29.7 5.7 %collective-permute-start.1 = (bf16[128,2048]{0,1:T(8,128)(2,1)S(1)}, bf16[128,2048]{0,1:T(8,128)(2,1)S(1)}, u32[]{:S(2)}, u32[]{:S(2)}) collective-permute-start(bf16[128,2048]{0,1:T(8,128)(2,1)S(1)} %collective-permute-done), channel_id=1, source_target_pairs={{0,1},{1,2},{2,3},{3,0},{4,5},{5,6},{6,7},{7,4},{8,9},{9,10},{10,1... | collective-permute-start | bytes 1572872 | tf_op jit(solution)/shard_map/ppermute | solution.py:69
  35.4 1.9 gather_fusion.3
  37.4 22.8 %collective-permute-done.1 = bf16[128,2048]{0,1:T(8,128)(2,1)S(1)} collective-permute-done((bf16[128,2048]{0,1:T(8,128)(2,1)S(1)}, bf16[128,2048]{0,1:T(8,128)(2,1)S(1)}, u32[]{:S(2)}, u32[]{:S(2)}) %collective-permute-start.1) | collective-permute-done | bytes 524320 | tf_op jit(solution)/shard_map/ppermute | solution.py:69
  60.2 10.9 %collective-permute-start.2 = (bf16[128,2048]{0,1:T(8,128)(2,1)S(1)}, bf16[128,2048]{0,1:T(8,128)(2,1)S(1)}, u32[]{:S(2)}, u32[]{:S(2)}) collective-permute-start(bf16[128,2048]{0,1:T(8,128)(2,1)S(1)} %collective-permute-done.1), channel_id=1, source_target_pairs={{0,1},{1,2},{2,3},{3,0},{4,5},{5,6},{6,7},{7,4},{8,9},{9,10},{10,1... | collective-permute-start | bytes 1572872 | tf_op jit(solution)/shard_map/ppermute | solution.py:69
  71.2 13.3 %collective-permute-done.2 = bf16[128,2048]{0,1:T(8,128)(2,1)S(1)} collective-permute-done((bf16[128,2048]{0,1:T(8,128)(2,1)S(1)}, bf16[128,2048]{0,1:T(8,128)(2,1)S(1)}, u32[]{:S(2)}, u32[]{:S(2)}) %collective-permute-start.2) | collective-permute-done | bytes 524320 | tf_op jit(solution)/shard_map/ppermute | solution.py:69
  84.6 0.1 constant_dynamic-update-slice_fusion.6
  84.7 0.1 constant_dynamic-update-slice_fusion.5
  84.7 0.1 constant_dynamic-update-slice_fusion.4
  84.8 0.1 constant_dynamic-update-slice_fusion.3
  84.9 0.1 constant_dynamic-update-slice_fusion.2
  85.0 0.1 constant_dynamic-update-slice_fusion.1
  85.0 0.1 constant_dynamic-update-slice_fusion
  85.1 1.5 constant_dynamic-slice_fusion
  86.6 3.5 copy.73
  90.1 8.6 %gather_fusion.5 = bf16[256,128,128]{2,1,0:T(8,128)(2,1)} fusion(bf16[128,64,128]{2,0,1:T(8,128)(2,1)S(1)} %copy.73, s32[1024]{0:T(1024)S(1)} %pad_clamp_fusion.2), kind=kCustom, calls=%fused_computation.5 | custom fusion | bytes 16778240 | tf_op jit(solution)/shard_map/gather | solution.py:20
  98.7 3.2 copy.64
  101.9 8.6 %gather_fusion.4 = bf16[256,128,128]{2,1,0:T(8,128)(2,1)} fusion(bf16[128,64,128]{2,0,1:T(8,128)(2,1)S(1)} %copy.64, s32[1024]{0:T(1024)S(1)} %pad_clamp_fusion.3), kind=kCustom, calls=%fused_computation.4 | custom fusion | bytes 16778240 | tf_op jit(solution)/shard_map/gather | solution.py:20
  110.6 24.3 %all-gather.8.cloned.1.call-done = bf16[256,128,128]{2,1,0:T(8,128)(2,1)} async-done(((bf16[64,128,128]{2,1,0:T(8,128)(2,1)}), bf16[256,128,128]{2,1,0:T(8,128)(2,1)}) %all-gather.8.cloned.1.call-update) | async-done | bytes 8388624 | tf_op jit(solution)/shard_map/all_gather | solution.py:51
  134.9 13.4 %gather_fusion.2 = bf16[256,128,128]{2,1,0:T(8,128)(2,1)} fusion(bf16[256,128,128]{2,1,0:T(8,128)(2,1)} %all-gather.8.cloned.1.call-done, s32[1024]{0:T(1024)S(1)} %pad_clamp_fusion.4), kind=kCustom, calls=%fused_computation.2 | custom fusion | bytes 16778240 | tf_op jit(solution)/shard_map/gather | solution.py:36
  148.3 8.4 %fusion.15 = f32[32,128,128,1]{2,1,3,0:T(8,128)S(1)} fusion(bf16[32,8,128,128]{3,2,1,0:T(8,128)(2,1)} %bitcast.97, bf16[128,32,8,128]{3,0,2,1:T(8,128)(2,1)} %bitcast.99), kind=kOutput, calls=%fused_computation.49 | convolution fusion | flops 1073741824 | bytes 18874368 | tf_op jit(solution)/shard_map/thkb,hkbc->thc/dot_general | solution.py:53
  156.7 9.3 %convolution_convert_fusion = bf16[32,8,128,128]{3,2,1,0:T(8,128)(2,1)} fusion(bf16[128,32,8,128]{3,0,2,1:T(8,128)(2,1)} %bitcast.106, f32[32,128,128,1]{2,1,3,0:T(8,128)S(1)} %fusion.15), kind=kOutput, calls=%fused_computation.10 | convolution fusion | flops 1080557568 | bytes 18874368 | tf_op jit(solution)/shard_map/thb,thkc->hkbc/dot_general | solution.py:90
  166.1 12.1 %gather_fusion.7 = bf16[256,128,128]{1,2,0:T(8,128)(2,1)} fusion(bf16[256,128,128]{1,2,0:T(8,128)(2,1)} %bitcast.113, s32[1024]{0:T(1024)S(1)} %get-tuple-element.24), kind=kCustom, calls=%fused_computation.7 | custom fusion | bytes 16778240 | tf_op jit(solution)/shard_map/gather | solution.py:96
  178.1 12.0 %copy.82 = bf16[4,2,32,128,128]{4,3,2,0,1:T(8,128)(2,1)} copy(bf16[4,2,32,128,128]{3,4,2,1,0:T(8,128)(2,1)} %bitcast.111) | data formatting | bytes 16777216 | tf_op jit(solution)/shard_map/convert_element_type | solution.py:110
  190.1 0.0 reduce-scatter.9.cloned.1.call-start
  190.2 4.6 all-gather.6.cloned.1.call-done
  194.8 12.7 %gather_fusion.1 = bf16[256,128,128]{2,1,0:T(8,128)(2,1)} fusion(bf16[256,128,128]{2,1,0:T(8,128)(2,1)} %all-gather.6.cloned.1.call-done, s32[1024]{0:T(1024)S(1)} %pad_clamp_fusion.5), kind=kCustom, calls=%fused_computation.1 | custom fusion | bytes 16778240 | tf_op jit(solution)/shard_map/gather | solution.py:36
  207.4 10.7 %fusion.10 = bf16[128,32,128,1]{0,2,3,1:T(8,128)(2,1)S(1)} fusion(f32[32,128,128,1]{2,1,3,0:T(8,128)S(1)} %fusion.15, bf16[32,8,128,128]{3,2,1,0:T(8,128)(2,1)} %bitcast.108, bf16[128,32,8,128]{3,0,2,1:T(8,128)(2,1)} %bitcast.107), kind=kOutput, calls=%fused_computation.25 | convolution fusion | flops 1078984704 | bytes 19922944 | tf_op jit(solution)/shard_map/thkc,hkbc->thb/dot_general | solution.py:76
  218.2 9.1 %convolution_convert_fusion.1 = bf16[32,8,128,128]{3,2,1,0:T(8,128)(2,1)} fusion(bf16[128,32,8,128]{3,0,2,1:T(8,128)(2,1)} %bitcast.100, bf16[128,32,128,1]{0,2,3,1:T(8,128)(2,1)S(1)} %fusion.10), kind=kOutput, calls=%fused_computation.11 | convolution fusion | flops 1077936128 | bytes 17825792 | tf_op jit(solution)/shard_map/thkb,thc->hkbc/dot_general | solution.py:87
  227.2 12.3 %gather_fusion.6 = bf16[256,128,128]{2,1,0:T(8,128)(2,1)} fusion(bf16[256,128,128]{2,1,0:T(8,128)(2,1)} %bitcast.110, s32[1024]{0:T(1024)S(1)} %get-tuple-element.25), kind=kCustom, calls=%fused_computation.6 | custom fusion | bytes 16778240 | tf_op jit(solution)/shard_map/gather | solution.py:95
  239.5 10.4 %copy.79 = bf16[4,2,32,128,128]{4,3,2,0,1:T(8,128)(2,1)} copy(bf16[4,2,32,128,128]{4,3,2,1,0:T(8,128)(2,1)} %bitcast.112) | data formatting | bytes 16777216 | tf_op jit(solution)/shard_map/convert_element_type | solution.py:107
  249.9 0.3 reduce-scatter.5.cloned.1.call-start
  250.2 11.6 %fusion.13 = f32[32,8,128,128]{3,2,1,0:T(8,128)} fusion(bf16[32,8,128,128]{3,2,1,0:T(8,128)(2,1)} %bitcast.109, f32[32,128,128,1]{2,1,3,0:T(8,128)S(1)} %fusion.15), kind=kOutput, calls=%fused_computation.48 | convolution fusion | flops 1076363264 | bytes 27262976 | tf_op jit(solution)/shard_map/thb,hkbc->thkc/dot_general | solution.py:60
  261.8 17.5 %copy.68 = f32[128,256,128]{2,0,1:T(8,128)} copy(f32[128,256,128]{0,2,1:T(8,128)} %bitcast.103) | data formatting | bytes 33554432 | tf_op jit(solution)/shard_map/reshape | solution.py:27
  279.3 2.9 broadcast.43.clone
  282.2 52.5 %scatter_fusion = f32[128,64,128]{2,0,1:T(8,128)} fusion(f32[128,64,128]{2,0,1:T(8,128)} %broadcast.43.clone, s32[256]{0:T(256)S(1)} %bitcast.121, f32[256,128,128]{2,1,0:T(8,128)} %bitcast.102), kind=kCustom, calls=%fused_computation.8 | custom fusion | flops 4194304 | bytes 50332672 | tf_op jit(solution)/shard_map/scatter-add | solution.py:29
  334.7 2.6 convert_element_type.64
  337.3 2.9 copy.69
  340.2 0.0 reduce-scatter.7.cloned.1.call-start
  340.3 11.5 %fusion.16 = f32[32,8,128,128]{3,2,1,0:T(8,128)} fusion(bf16[32,8,128,128]{3,2,1,0:T(8,128)(2,1)} %bitcast.98, bf16[128,32,128,1]{0,2,3,1:T(8,128)(2,1)S(1)} %fusion.10), kind=kOutput, calls=%fused_computation.50 | convolution fusion | flops 1073741824 | bytes 26214400 | tf_op jit(solution)/shard_map/thc,hkbc->thkb/dot_general | solution.py:80
  351.8 17.6 %copy.75 = f32[128,256,128]{2,0,1:T(8,128)} copy(f32[128,256,128]{0,2,1:T(8,128)} %bitcast.96) | data formatting | bytes 33554432 | tf_op jit(solution)/shard_map/reshape | solution.py:27
  369.4 2.5 broadcast.43.clone.1
  371.9 51.3 %scatter_fusion.1 = f32[128,64,128]{2,0,1:T(8,128)} fusion(f32[128,64,128]{2,0,1:T(8,128)} %broadcast.43.clone.1, s32[256]{0:T(256)S(1)} %bitcast.119, f32[256,128,128]{2,1,0:T(8,128)} %bitcast.101), kind=kCustom, calls=%fused_computation.9 | custom fusion | flops 4194304 | bytes 50332672 | tf_op jit(solution)/shard_map/scatter-add | solution.py:29
  423.2 2.6 convert_element_type.67
  425.8 2.9 copy.76
  428.8 0.7 all-gather.14.cloned.1.call-update
  429.5 0.7 all-gather.12.cloned.1.call-update
  430.2 2.0 copy.83
  432.2 40.6 %reduce-scatter.7.cloned.1.call-done = bf16[128,2048]{0,1:T(8,128)(2,1)} async-done(((bf16[128,8192]{0,1:T(8,128)(2,1)}), bf16[128,2048]{0,1:T(8,128)(2,1)}) %reduce-scatter.7.cloned.1.call-update) | async-done | bytes 524304 | tf_op jit(solution)/shard_map/reduce_scatter | solution.py:84
  472.8 2.0 copy.84
  474.9 31.9 %all-gather.14.cloned.1.call-done = bf16[64,128,128]{2,1,0:T(8,128)(2,1)} async-done(((bf16[32,128,128]{2,1,0:T(8,128)(2,1)}), bf16[64,128,128]{2,1,0:T(8,128)(2,1)}) %all-gather.14.cloned.1.call-update) | async-done | bytes 2097168 | tf_op jit(solution)/shard_map/all_gather | solution.py:117
  506.7 4.1 convert_element_type.79
  510.9 30.5 %all-gather.12.cloned.1.call-done = bf16[64,128,128]{2,1,0:T(8,128)(2,1)} async-done(((bf16[32,128,128]{2,1,0:T(8,128)(2,1)}), bf16[64,128,128]{2,1,0:T(8,128)(2,1)}) %all-gather.12.cloned.1.call-update) | async-done | bytes 2097168 | tf_op jit(solution)/shard_map/all_gather | solution.py:114
  541.4 4.1 convert_element_type.73
  (43 shorter events, 0.5 us)
Async XLA Ops:
  7.2 19.9 %copy-start = (s32[256,1]{0,1:T(1,128)S(1)}, s32[256,1]{0,1:T(1,128)}, u32[]{:S(2)}) copy-start(s32[256,1]{0,1:T(1,128)} %param.15) | copy-start | bytes 3076
  7.2 3.7 copy-start.3
  7.2 7.1 %copy-start.4 = (s32[256,1]{0,1:T(1,128)S(1)}, s32[256,1]{0,1:T(1,128)}, u32[]{:S(2)}) copy-start(s32[256,1]{0,1:T(1,128)} %param.14) | copy-start | bytes 3076
  7.2 13.5 %copy-start.5 = (s32[256,1]{0,1:T(1,128)S(1)}, s32[256,1]{0,1:T(1,128)}, u32[]{:S(2)}) copy-start(s32[256,1]{0,1:T(1,128)} %param.13) | copy-start | bytes 3076
  7.2 28.2 %copy-start.2 = (s32[256,1]{0,1:T(1,128)S(1)}, s32[256,1]{0,1:T(1,128)}, u32[]{:S(2)}) copy-start(s32[256,1]{0,1:T(1,128)} %param.12) | copy-start | bytes 3076
  7.2 91.5 %all-gather.10.cloned.1.call-start = ((), (), s32[]{:S(2)}) async-start(), calls=%async_computation.6 | async-start | bytes 2621440 | tf_op jit(solution)/shard_map/all_gather | solution.py:49
  9.4 125.5 %all-gather.8.cloned.1.call-start = ((), (), s32[]{:S(2)}) async-start(), calls=%async_computation.5 | async-start | bytes 10485760 | tf_op jit(solution)/shard_map/all_gather | solution.py:51
  10.1 184.6 %all-gather.6.cloned.1.call-start = ((), (), s32[]{:S(2)}) async-start(), calls=%async_computation.4 | async-start | bytes 10485760 | tf_op jit(solution)/shard_map/all_gather | solution.py:58
  10.9 417.9 %reduce-scatter.11.cloned.1.call-start = ((), (), s32[]{:S(2)}) async-start(), calls=%async_computation.11 | async-start | bytes 9437184 | tf_op jit(solution)/shard_map/reduce_scatter | solution.py:109
  11.2 18.5 %collective-permute-start = (bf16[128,2048]{0,1:T(8,128)(2,1)S(1)}, bf16[128,2048]{0,1:T(8,128)(2,1)S(1)}, u32[]{:S(2)}, u32[]{:S(2)}) collective-permute-start(bf16[128,2048]{0,1:T(8,128)(2,1)S(1)} %copy.70), channel_id=1, source_target_pairs={{0,1},{1,2},{2,3},{3,0},{4,5},{5,6},{6,7},{7,4},{8,9},{9,10},{10,1... | collective-permute-start | bytes 1572872 | tf_op jit(solution)/shard_map/ppermute | solution.py:69
  29.7 30.5 %collective-permute-start.1 = (bf16[128,2048]{0,1:T(8,128)(2,1)S(1)}, bf16[128,2048]{0,1:T(8,128)(2,1)S(1)}, u32[]{:S(2)}, u32[]{:S(2)}) collective-permute-start(bf16[128,2048]{0,1:T(8,128)(2,1)S(1)} %collective-permute-done), channel_id=1, source_target_pairs={{0,1},{1,2},{2,3},{3,0},{4,5},{5,6},{6,7},{7,4},{8,9},{9,10},{10,1... | collective-permute-start | bytes 1572872 | tf_op jit(solution)/shard_map/ppermute | solution.py:69
  60.2 24.3 %collective-permute-start.2 = (bf16[128,2048]{0,1:T(8,128)(2,1)S(1)}, bf16[128,2048]{0,1:T(8,128)(2,1)S(1)}, u32[]{:S(2)}, u32[]{:S(2)}) collective-permute-start(bf16[128,2048]{0,1:T(8,128)(2,1)S(1)} %collective-permute-done.1), channel_id=1, source_target_pairs={{0,1},{1,2},{2,3},{3,0},{4,5},{5,6},{6,7},{7,4},{8,9},{9,10},{10,1... | collective-permute-start | bytes 1572872 | tf_op jit(solution)/shard_map/ppermute | solution.py:69
  190.1 239.4 %reduce-scatter.9.cloned.1.call-start = ((), (), s32[]{:S(2)}) async-start(), calls=%async_computation.9 | async-start | bytes 9437184 | tf_op jit(solution)/shard_map/reduce_scatter | solution.py:106
  249.9 180.3 %reduce-scatter.5.cloned.1.call-start = ((), (), s32[]{:S(2)}) async-start(), calls=%async_computation.7 | async-start | bytes 2621440 | tf_op jit(solution)/shard_map/reduce_scatter | solution.py:64
  340.2 132.6 %reduce-scatter.7.cloned.1.call-start = ((), (), s32[]{:S(2)}) async-start(), calls=%async_computation.8 | async-start | bytes 2621440 | tf_op jit(solution)/shard_map/reduce_scatter | solution.py:84
  428.7 78.0 %all-gather.14.cloned.1.call-start = ((), (), s32[]{:S(2)}) async-start(), calls=%async_computation.12 | async-start | bytes 3145728 | tf_op jit(solution)/shard_map/all_gather | solution.py:117
  429.4 112.0 %all-gather.12.cloned.1.call-start = ((), (), s32[]{:S(2)}) async-start(), calls=%async_computation.10 | async-start | bytes 3145728 | tf_op jit(solution)/shard_map/all_gather | solution.py:114
  506.7 38.8 %copy-start.1 = (s32[256,1]{0,1:T(1,128)S(1)}, s32[256,1]{0,1:T(1,128)}, u32[]{:S(2)}) copy-start(s32[256,1]{0,1:T(1,128)} %param.15) | copy-start | bytes 3076
Sparse Core Ops, SparseCore 0:
  10.2 65.2 all-gather.9
  77.1 57.7 all-gather.7
  136.5 58.2 all-gather.5
  198.1 71.4 reduce-scatter.10
  272.9 71.4 reduce-scatter.8
  347.2 43.6 reduce-scatter.4
  428.8 43.9 reduce-scatter.6
  474.4 32.3 all-gather.13
  508.3 33.0 all-gather.11
